TPU v7x, 256 devices: a whole 4x4x8 slice. The times are simulated.
256 devices in a mesh: clique: 8 (over y_hi, x), copy: 32 (over z, y_lo, core).
Axes of the slice: x: 4, y: 4 (y_hi: 2, y_lo: 2; y = y_hi * 2 + y_lo), z: 8, core: 2. Of those that a mesh axis runs over, the one named last changes fastest.
Arguments:
- out_grad: bfloat16 [524288, 512], P(('clique', 'copy')), may hold values from -6 to 6
- pre_act: bfloat16 [524288, 512], P(('clique', 'copy')), may hold values from -6 to 6
- batch_count: int32 [256], P(('clique', 'copy')), may hold values from 1024 to 2048, as said below
- layer_two: bfloat16 [512, 512], replicated, may hold values from -0.25 to 0.25
- hot_slots: int32 [524288, 10], P(('clique', 'copy')), may hold values from 0 to 4095
- cold_index: int32 [524288, 15], P(('clique', 'copy')), may hold values from 0 to 2047
- hot_feats: bfloat16 [4096, 768], P('clique'), may hold values from -6 to 6
- cold_feats: bfloat16 [524288, 768], P(('clique', 'copy')), may hold values from -6 to 6
Outputs:
- grad_one: float32 [768, 512], replicated
- grad_two: float32 [512, 512], replicated
Inputs may be any that keep to these rules, and one draw needn't show every extreme that they name: `batch_count`: some device has all 2048 rows live in every draw.
All inputs are finite; a program needn't handle non-finite values.
Results may differ from a plain program's by a relative error of at most 0.015.
Values may be sent and summed in bfloat16 or wider, within the bound.
A program may use at most 128 MiB of HBM per device.

v0:
```python
import jax
import jax.numpy as jnp
from jax import lax
from jax.sharding import PartitionSpec as P


def table_sums(index_cols, row_grad, table_rows, fanout):
    block = min(512, table_rows)
    blocks = table_rows // block
    offsets = jnp.arange(block, dtype=jnp.int32)

    def one_block(start):
        wanted = start + offsets
        counts = jnp.zeros((block, index_cols.shape[0]), jnp.float32)
        for column in range(index_cols.shape[1]):
            counts = counts + (index_cols[:, column][None, :] == wanted[:, None]).astype(
                jnp.float32
            )
        summed = jnp.dot(counts.astype(jnp.bfloat16), row_grad, preferred_element_type=jnp.float32)
        return (summed * (1.0 / fanout)).astype(jnp.bfloat16)

    starts = jnp.arange(blocks, dtype=jnp.int32) * block
    parts = lax.map(one_block, starts)
    return parts.reshape(table_rows, row_grad.shape[1])


def on_device(
    out_grad, pre_act, batch_count, layer_two, hot_slots, cold_index, hot_feats, cold_feats
):
    rows = out_grad.shape[0]
    hot_local = hot_feats.shape[0]
    hot_total = hot_local * lax.axis_size("clique")
    k_hot = hot_slots.shape[1]
    k_cold = cold_index.shape[1]
    fanout = k_hot + k_cold
    cold_rows = cold_feats.shape[0]
    live = (jnp.arange(rows, dtype=jnp.int32) < batch_count[0])[:, None]
    masked = jnp.where(live, out_grad, jnp.zeros_like(out_grad))
    activ = jnp.maximum(pre_act, jnp.zeros_like(pre_act))
    grad_two = jnp.dot(activ.T, masked, preferred_element_type=jnp.float32)
    back = jnp.dot(masked, layer_two.T, preferred_element_type=jnp.float32)
    row_grad = jnp.where(pre_act > 0, back, jnp.zeros_like(back)).astype(jnp.bfloat16)
    hot_part = table_sums(hot_slots, row_grad, hot_total, fanout)
    summed = lax.psum(hot_part, "clique").astype(jnp.float32)
    owned = lax.dynamic_slice_in_dim(summed, lax.axis_index("clique") * hot_local, hot_local, 0)
    cold_part = table_sums(cold_index, row_grad, cold_rows, fanout)
    grad_one = jnp.dot(cold_feats.T, cold_part, preferred_element_type=jnp.float32)
    grad_one = grad_one + jnp.dot(
        hot_feats.T, owned.astype(jnp.bfloat16), preferred_element_type=jnp.float32
    )
    total_one, total_two = lax.psum((grad_one, grad_two), ("clique", "copy"))
    return (total_one, total_two)


def solution(mesh):
    placed = (
        P(("clique", "copy"), None),
        P(("clique", "copy"), None),
        P(("clique", "copy")),
        P(),
        P(("clique", "copy"), None),
        P(("clique", "copy"), None),
        P("clique", None),
        P(("clique", "copy"), None),
    )
    return jax.shard_map(
        on_device, mesh=mesh, in_specs=placed, out_specs=(P(), P()), check_vma=False
    )
```

profile of v0, /device:TPU:2, one launch (start us, length us, event | category | flops | bytes accessed | tf_op | source)
XLA Modules:
  0.0 475.0 jit_solution(12058573302038147682)
XLA Ops:
  8.1 5.2 %select_convert_fusion = bf16[2048,512]{1,0:T(8,128)(2,1)} fusion(bf16[2048,512]{1,0:T(8,128)(2,1)} %param.13, bf16[512,512]{1,0:T(8,128)(2,1)} %param.15, bf16[2048,512]{1,0:T(8,128)(2,1)} %param.12, pred[2048]{0:T(1024)(128)(4,1)S(1)} %iota_compare_fusion), kind=kOutput, calls=%fused_computation.43 | convolution fusion | flops 1077936128 | bytes 6817792 | tf_op jit(solution)/shard_map/dot_general | solution.py:41
  13.2 63.4 %while.23 = (s32[]{:T(128)}, bf16[8,512,512]{2,1,0:T(8,128)(2,1)}, s32[2048,10]{0,1:T(8,128)S(1)}, s32[8]{0:T(128)S(1)}, bf16[2048,512]{1,0:T(8,128)(2,1)}, /*index=5*/s32[]{:T(128)}) while((s32[]{:T(128)}, bf16[8,512,512]{2,1,0:T(8,128)(2,1)}, s32[2048,10]{0,1:T(8,128)S(1)}, s32[8]{0:T(128)S(1)}, bf16[2048,512]{1,0:T(8,128)(2,1)}, ...), condition=%wide.region_3.4_spmd.clone, body=%wide.region_2.3_spmd.clone.sunk | while | flops 1105723904 | bytes 2871893 | solution.py:23
  13.3 0.6 dynamic_slice.22
  14.6 6.6 %fusion.68 = bf16[8,512,512]{2,1,0:T(8,128)(2,1)} fusion(bf16[8,512,512]{2,1,0:T(8,128)(2,1)} %get-tuple-element.278, s32[]{:T(128)} %get-tuple-element.277, bf16[2048,512]{1,0:T(8,128)(2,1)} %get-tuple-element.287, s32[2048]{0:T(1024)S(1)} %bitcast.126, s32[2048]{0:T(1024)S(1)} %bitcast.127, s32[2048]{0:T(1024)S(1)} %bitcast.128, ...), kind=kOutput, calls=%fused_computation.41.clone.1 | convolution fusion | flops 1105723392 | bytes 2705920 | tf_op jit(solution)/shard_map/while/body/eval_jaxpr/dot_general | solution.py:19
  21.2 0.6 dynamic_slice.22
  22.5 6.6 %fusion.68 = bf16[8,512,512]{2,1,0:T(8,128)(2,1)} fusion(bf16[8,512,512]{2,1,0:T(8,128)(2,1)} %get-tuple-element.278, s32[]{:T(128)} %get-tuple-element.277, bf16[2048,512]{1,0:T(8,128)(2,1)} %get-tuple-element.287, s32[2048]{0:T(1024)S(1)} %bitcast.126, s32[2048]{0:T(1024)S(1)} %bitcast.127, s32[2048]{0:T(1024)S(1)} %bitcast.128, ...), kind=kOutput, calls=%fused_computation.41.clone.1 | convolution fusion | flops 1105723392 | bytes 2705920 | tf_op jit(solution)/shard_map/while/body/eval_jaxpr/dot_general | solution.py:19
  29.2 0.6 dynamic_slice.22
  30.4 6.6 %fusion.68 = bf16[8,512,512]{2,1,0:T(8,128)(2,1)} fusion(bf16[8,512,512]{2,1,0:T(8,128)(2,1)} %get-tuple-element.278, s32[]{:T(128)} %get-tuple-element.277, bf16[2048,512]{1,0:T(8,128)(2,1)} %get-tuple-element.287, s32[2048]{0:T(1024)S(1)} %bitcast.126, s32[2048]{0:T(1024)S(1)} %bitcast.127, s32[2048]{0:T(1024)S(1)} %bitcast.128, ...), kind=kOutput, calls=%fused_computation.41.clone.1 | convolution fusion | flops 1105723392 | bytes 2705920 | tf_op jit(solution)/shard_map/while/body/eval_jaxpr/dot_general | solution.py:19
  37.1 0.6 dynamic_slice.22
  38.4 6.6 %fusion.68 = bf16[8,512,512]{2,1,0:T(8,128)(2,1)} fusion(bf16[8,512,512]{2,1,0:T(8,128)(2,1)} %get-tuple-element.278, s32[]{:T(128)} %get-tuple-element.277, bf16[2048,512]{1,0:T(8,128)(2,1)} %get-tuple-element.287, s32[2048]{0:T(1024)S(1)} %bitcast.126, s32[2048]{0:T(1024)S(1)} %bitcast.127, s32[2048]{0:T(1024)S(1)} %bitcast.128, ...), kind=kOutput, calls=%fused_computation.41.clone.1 | convolution fusion | flops 1105723392 | bytes 2705920 | tf_op jit(solution)/shard_map/while/body/eval_jaxpr/dot_general | solution.py:19
  45.0 0.6 dynamic_slice.22
  46.3 6.6 %fusion.68 = bf16[8,512,512]{2,1,0:T(8,128)(2,1)} fusion(bf16[8,512,512]{2,1,0:T(8,128)(2,1)} %get-tuple-element.278, s32[]{:T(128)} %get-tuple-element.277, bf16[2048,512]{1,0:T(8,128)(2,1)} %get-tuple-element.287, s32[2048]{0:T(1024)S(1)} %bitcast.126, s32[2048]{0:T(1024)S(1)} %bitcast.127, s32[2048]{0:T(1024)S(1)} %bitcast.128, ...), kind=kOutput, calls=%fused_computation.41.clone.1 | convolution fusion | flops 1105723392 | bytes 2705920 | tf_op jit(solution)/shard_map/while/body/eval_jaxpr/dot_general | solution.py:19
  52.9 0.6 dynamic_slice.22
  54.2 6.6 %fusion.68 = bf16[8,512,512]{2,1,0:T(8,128)(2,1)} fusion(bf16[8,512,512]{2,1,0:T(8,128)(2,1)} %get-tuple-element.278, s32[]{:T(128)} %get-tuple-element.277, bf16[2048,512]{1,0:T(8,128)(2,1)} %get-tuple-element.287, s32[2048]{0:T(1024)S(1)} %bitcast.126, s32[2048]{0:T(1024)S(1)} %bitcast.127, s32[2048]{0:T(1024)S(1)} %bitcast.128, ...), kind=kOutput, calls=%fused_computation.41.clone.1 | convolution fusion | flops 1105723392 | bytes 2705920 | tf_op jit(solution)/shard_map/while/body/eval_jaxpr/dot_general | solution.py:19
  60.9 0.6 dynamic_slice.22
  62.1 6.6 %fusion.68 = bf16[8,512,512]{2,1,0:T(8,128)(2,1)} fusion(bf16[8,512,512]{2,1,0:T(8,128)(2,1)} %get-tuple-element.278, s32[]{:T(128)} %get-tuple-element.277, bf16[2048,512]{1,0:T(8,128)(2,1)} %get-tuple-element.287, s32[2048]{0:T(1024)S(1)} %bitcast.126, s32[2048]{0:T(1024)S(1)} %bitcast.127, s32[2048]{0:T(1024)S(1)} %bitcast.128, ...), kind=kOutput, calls=%fused_computation.41.clone.1 | convolution fusion | flops 1105723392 | bytes 2705920 | tf_op jit(solution)/shard_map/while/body/eval_jaxpr/dot_general | solution.py:19
  68.8 0.6 dynamic_slice.22
  70.1 6.6 %fusion.68 = bf16[8,512,512]{2,1,0:T(8,128)(2,1)} fusion(bf16[8,512,512]{2,1,0:T(8,128)(2,1)} %get-tuple-element.278, s32[]{:T(128)} %get-tuple-element.277, bf16[2048,512]{1,0:T(8,128)(2,1)} %get-tuple-element.287, s32[2048]{0:T(1024)S(1)} %bitcast.126, s32[2048]{0:T(1024)S(1)} %bitcast.127, s32[2048]{0:T(1024)S(1)} %bitcast.128, ...), kind=kOutput, calls=%fused_computation.41.clone.1 | convolution fusion | flops 1105723392 | bytes 2705920 | tf_op jit(solution)/shard_map/while/body/eval_jaxpr/dot_general | solution.py:19
  77.0 4.6 fusion.41
  81.5 39.8 %while.22 = (s32[]{:T(128)}, bf16[4,512,512]{2,1,0:T(8,128)(2,1)}, s32[2048,15]{0,1:T(8,128)S(1)}, s32[4]{0:T(128)S(1)}, bf16[2048,512]{1,0:T(8,128)(2,1)}, /*index=5*/s32[]{:T(128)}) while((s32[]{:T(128)}, bf16[4,512,512]{2,1,0:T(8,128)(2,1)}, s32[2048,15]{0,1:T(8,128)S(1)}, s32[4]{0:T(128)S(1)}, bf16[2048,512]{1,0:T(8,128)(2,1)}, ...), condition=%wide.region_1.2_spmd.clone, body=%wide.region_0.1_spmd.clone.sunk | while | flops 1121452544 | bytes 2994773 | solution.py:23
  82.2 0.6 iota_add_fusion.4
  82.9 8.6 %fusion.65 = bf16[4,512,512]{2,1,0:T(8,128)(2,1)} fusion(bf16[4,512,512]{2,1,0:T(8,128)(2,1)} %get-tuple-element.260, s32[]{:T(128)} %get-tuple-element.259, bf16[2048,512]{1,0:T(8,128)(2,1)} %get-tuple-element.269, s32[2048]{0:T(1024)S(1)} %bitcast.111, s32[2048]{0:T(1024)S(1)} %bitcast.112, s32[2048]{0:T(1024)S(1)} %bitcast.113, ...), kind=kOutput, calls=%fused_computation.23.clone.1 | convolution fusion | flops 1121452032 | bytes 2746880 | tf_op jit(solution)/shard_map/while/body/eval_jaxpr/dot_general | solution.py:19
  92.2 0.6 iota_add_fusion.4
  92.9 8.6 %fusion.65 = bf16[4,512,512]{2,1,0:T(8,128)(2,1)} fusion(bf16[4,512,512]{2,1,0:T(8,128)(2,1)} %get-tuple-element.260, s32[]{:T(128)} %get-tuple-element.259, bf16[2048,512]{1,0:T(8,128)(2,1)} %get-tuple-element.269, s32[2048]{0:T(1024)S(1)} %bitcast.111, s32[2048]{0:T(1024)S(1)} %bitcast.112, s32[2048]{0:T(1024)S(1)} %bitcast.113, ...), kind=kOutput, calls=%fused_computation.23.clone.1 | convolution fusion | flops 1121452032 | bytes 2746880 | tf_op jit(solution)/shard_map/while/body/eval_jaxpr/dot_general | solution.py:19
  102.8 8.6 %fusion.65 = bf16[4,512,512]{2,1,0:T(8,128)(2,1)} fusion(bf16[4,512,512]{2,1,0:T(8,128)(2,1)} %get-tuple-element.260, s32[]{:T(128)} %get-tuple-element.259, bf16[2048,512]{1,0:T(8,128)(2,1)} %get-tuple-element.269, s32[2048]{0:T(1024)S(1)} %bitcast.111, s32[2048]{0:T(1024)S(1)} %bitcast.112, s32[2048]{0:T(1024)S(1)} %bitcast.113, ...), kind=kOutput, calls=%fused_computation.23.clone.1 | convolution fusion | flops 1121452032 | bytes 2746880 | tf_op jit(solution)/shard_map/while/body/eval_jaxpr/dot_general | solution.py:19
  112.8 8.6 %fusion.65 = bf16[4,512,512]{2,1,0:T(8,128)(2,1)} fusion(bf16[4,512,512]{2,1,0:T(8,128)(2,1)} %get-tuple-element.260, s32[]{:T(128)} %get-tuple-element.259, bf16[2048,512]{1,0:T(8,128)(2,1)} %get-tuple-element.269, s32[2048]{0:T(1024)S(1)} %bitcast.111, s32[2048]{0:T(1024)S(1)} %bitcast.112, s32[2048]{0:T(1024)S(1)} %bitcast.113, ...), kind=kOutput, calls=%fused_computation.23.clone.1 | convolution fusion | flops 1121452032 | bytes 2746880 | tf_op jit(solution)/shard_map/while/body/eval_jaxpr/dot_general | solution.py:19
  121.4 4.6 fusion.50
  126.0 66.5 %all-reduce.4.cloned.1.call-done = bf16[4096,512]{1,0:T(8,128)(2,1)} async-done(((bf16[4096,512]{1,0:T(8,128)(2,1)}), bf16[4096,512]{1,0:T(8,128)(2,1)}) %all-reduce.4.cloned.1.call-update) | async-done | bytes 4194320 | tf_op jit(solution)/shard_map/psum | solution.py:44
  192.5 3.6 add_bitcast_fusion
  196.0 266.8 %all-reduce.6.cloned.1.call-done = (f32[768,512]{0,1:T(8,128)}, f32[512,512]{1,0:T(8,128)}) async-done(((f32[768,512]{0,1:T(8,128)}, f32[512,512]{1,0:T(8,128)}), (f32[768,512]{0,1:T(8,128)}, f32[512,512]{1,0:T(8,128)})) %all-reduce.6.cloned.1.call-update) | async-done | bytes 2621456 | tf_op jit(solution)/shard_map/psum | solution.py:51
  462.9 3.0 copy.10
  465.9 2.3 copy.30
  (41 shorter events, 9.8 us)
Async XLA Ops:
  7.2 114.2 %copy-start = (bf16[2048,768]{1,0:T(8,128)(2,1)S(1)}, bf16[2048,768]{1,0:T(8,128)(2,1)}, u32[]{:S(2)}) copy-start(bf16[2048,768]{1,0:T(8,128)(2,1)} %param.19) | copy-start | bytes 9437188
  7.2 185.3 %all-reduce.4.cloned.1.call-start = ((), (), s32[]{:S(2)}) async-start(), calls=%async_computation | async-start | bytes 8388608 | tf_op jit(solution)/shard_map/psum | solution.py:44
  8.1 5.2 %copy-start.2 = (s32[2048,10]{0,1:T(8,128)S(1)}, s32[2048,10]{0,1:T(8,128)}, u32[]{:S(2)}) copy-start(s32[2048,10]{0,1:T(8,128)} %param.16) | copy-start | bytes 245764
  76.7 4.8 %copy-start.1 = (s32[2048,15]{0,1:T(8,128)S(1)}, s32[2048,15]{0,1:T(8,128)}, u32[]{:S(2)}) copy-start(s32[2048,15]{0,1:T(8,128)} %param.17) | copy-start | bytes 368644
  76.7 386.1 %all-reduce.6.cloned.1.call-start = ((), (), s32[]{:S(2)}) async-start(), calls=%async_computation.1 | async-start | bytes 5242880 | tf_op jit(solution)/shard_map/psum | solution.py:51
Sparse Core Ops, SparseCore 0:
  76.8 115.5 all-reduce.3
  198.6 264.2 all-reduce.5
where the time goes:
time: 476 us; the launch traced here: 475 us
  waiting for transfers between devices  333 us (70%)
  matrix products  105 us (22%)
  between operations  14.9 us (3%)
  local copies, waits for them, and re-layouts  13.6 us (3%)
  other arithmetic  7.56 us (2%)
    psum x1, waiting for transfers between devices, on_device(): total_one, total_two = lax.psum((grad_one, grad_two), ('clique', 'copy'))  267 us
    dot_general x12, matrix products, one_block(): jnp.dot(counts.astype(jnp.bfloat16), row_grad, preferred_element_type=jnp...  87.3 us
    psum x1, waiting for transfers between devices, on_device(): summed = lax.psum(hot_part, 'clique').astype(jnp.float32)  66.5 us
  transfers between devices with their start and end apart: 2, of which 2 were waited for; matrix products, arithmetic and copies ran while one was open for 10% of the time, Pallas kernels for 0%

commit v1 on v0

--- a/solution.py
+++ b/solution.py
@@ -2,6 +2,11 @@
 import jax.numpy as jnp
 from jax import lax
 from jax.sharding import PartitionSpec as P
+
+
+def move_slot(sheet, device_axis, mesh_ax="copy"):
+    res = lax.psum(sheet, axis_name=device_axis)
+    return lax.psum(res, axis_name=mesh_ax)
 
 
 def table_sums(index_cols, row_grad, table_rows, fanout):
@@ -48,7 +53,7 @@
     grad_one = grad_one + jnp.dot(
         hot_feats.T, owned.astype(jnp.bfloat16), preferred_element_type=jnp.float32
     )
-    total_one, total_two = lax.psum((grad_one, grad_two), ("clique", "copy"))
+    total_one, total_two = move_slot((grad_one, grad_two), device_axis="clique")
     return (total_one, total_two)
 
 

time: 476 us -> 547 us (1.15)
  waiting for transfers between devices: 333 us -> 403 us
    psum x1 -> x2, waiting for transfers between devices: 267 us -> 337 us  [the longest x1 237 us: move_slot(): return lax.psum(res, axis_name=mesh_ax)]
  transfers between devices with their start and end apart: 2 -> 3, of which waited for: 2 -> 3; matrix products, arithmetic and copies ran while one was open for 10% -> 9% of each run, Pallas kernels for 0% -> 0%
where the time goes in v1:
time: 547 us; the launch traced here: 545 us
  waiting for transfers between devices  403 us (74%)
  matrix products  105 us (19%)
  between operations  14.6 us (3%)
  local copies, waits for them, and re-layouts  13.7 us (3%)
  other arithmetic  7.46 us (1%)
    psum x1, waiting for transfers between devices, move_slot(): return lax.psum(res, axis_name=mesh_ax)  237 us
    psum x1, waiting for transfers between devices, move_slot(): res = lax.psum(sheet, axis_name=device_axis)  99.7 us
    dot_general x12, matrix products, one_block(): jnp.dot(counts.astype(jnp.bfloat16), row_grad, preferred_element_type=jnp...  87.3 us
    psum x1, waiting for transfers between devices, on_device(): summed = lax.psum(hot_part, 'clique').astype(jnp.float32)  66.6 us
  transfers between devices with their start and end apart: 3, of which 3 were waited for; matrix products, arithmetic and copies ran while one was open for 9% of the time, Pallas kernels for 0%

profile of v1, /device:TPU:2, one launch (start us, length us, event | category | flops | bytes accessed | tf_op | source)
XLA Modules:
  0.0 544.8 jit_solution(13814576440545793151)
XLA Ops:
  8.1 5.2 select_convert_fusion
  13.3 63.5 %while.23 = (s32[]{:T(128)}, bf16[8,512,512]{2,1,0:T(8,128)(2,1)}, s32[2048,10]{0,1:T(8,128)S(1)}, s32[8]{0:T(128)S(1)}, bf16[2048,512]{1,0:T(8,128)(2,1)}, /*index=5*/s32[]{:T(128)}) while((s32[]{:T(128)}, bf16[8,512,512]{2,1,0:T(8,128)(2,1)}, s32[2048,10]{0,1:T(8,128)S(1)}, s32[8]{0:T(128)S(1)}, bf16[2048,512]{1,0:T(8,128)(2,1)}, ...), condition=%wide.region_3.4_spmd.clone, body=%wide.region_2.3_spmd.clone.sunk | while | flops 1105723904 | bytes 2871893 | solution.py:28
  13.3 0.7 dynamic_slice.22
  14.6 6.6 %fusion.68 = bf16[8,512,512]{2,1,0:T(8,128)(2,1)} fusion(bf16[8,512,512]{2,1,0:T(8,128)(2,1)} %get-tuple-element.280, s32[]{:T(128)} %get-tuple-element.279, bf16[2048,512]{1,0:T(8,128)(2,1)} %get-tuple-element.289, s32[2048]{0:T(1024)S(1)} %bitcast.126, s32[2048]{0:T(1024)S(1)} %bitcast.127, s32[2048]{0:T(1024)S(1)} %bitcast.128, ...), kind=kOutput, calls=%fused_computation.41.clone.1 | convolution fusion | flops 1105723392 | bytes 2705920 | tf_op jit(solution)/shard_map/while/body/eval_jaxpr/dot_general | solution.py:24
  21.2 0.7 dynamic_slice.22
  22.5 6.6 %fusion.68 = bf16[8,512,512]{2,1,0:T(8,128)(2,1)} fusion(bf16[8,512,512]{2,1,0:T(8,128)(2,1)} %get-tuple-element.280, s32[]{:T(128)} %get-tuple-element.279, bf16[2048,512]{1,0:T(8,128)(2,1)} %get-tuple-element.289, s32[2048]{0:T(1024)S(1)} %bitcast.126, s32[2048]{0:T(1024)S(1)} %bitcast.127, s32[2048]{0:T(1024)S(1)} %bitcast.128, ...), kind=kOutput, calls=%fused_computation.41.clone.1 | convolution fusion | flops 1105723392 | bytes 2705920 | tf_op jit(solution)/shard_map/while/body/eval_jaxpr/dot_general | solution.py:24
  29.2 0.7 dynamic_slice.22
  30.5 6.6 %fusion.68 = bf16[8,512,512]{2,1,0:T(8,128)(2,1)} fusion(bf16[8,512,512]{2,1,0:T(8,128)(2,1)} %get-tuple-element.280, s32[]{:T(128)} %get-tuple-element.279, bf16[2048,512]{1,0:T(8,128)(2,1)} %get-tuple-element.289, s32[2048]{0:T(1024)S(1)} %bitcast.126, s32[2048]{0:T(1024)S(1)} %bitcast.127, s32[2048]{0:T(1024)S(1)} %bitcast.128, ...), kind=kOutput, calls=%fused_computation.41.clone.1 | convolution fusion | flops 1105723392 | bytes 2705920 | tf_op jit(solution)/shard_map/while/body/eval_jaxpr/dot_general | solution.py:24
  37.1 0.7 dynamic_slice.22
  38.4 6.6 %fusion.68 = bf16[8,512,512]{2,1,0:T(8,128)(2,1)} fusion(bf16[8,512,512]{2,1,0:T(8,128)(2,1)} %get-tuple-element.280, s32[]{:T(128)} %get-tuple-element.279, bf16[2048,512]{1,0:T(8,128)(2,1)} %get-tuple-element.289, s32[2048]{0:T(1024)S(1)} %bitcast.126, s32[2048]{0:T(1024)S(1)} %bitcast.127, s32[2048]{0:T(1024)S(1)} %bitcast.128, ...), kind=kOutput, calls=%fused_computation.41.clone.1 | convolution fusion | flops 1105723392 | bytes 2705920 | tf_op jit(solution)/shard_map/while/body/eval_jaxpr/dot_general | solution.py:24
  45.0 0.7 dynamic_slice.22
  46.3 6.6 %fusion.68 = bf16[8,512,512]{2,1,0:T(8,128)(2,1)} fusion(bf16[8,512,512]{2,1,0:T(8,128)(2,1)} %get-tuple-element.280, s32[]{:T(128)} %get-tuple-element.279, bf16[2048,512]{1,0:T(8,128)(2,1)} %get-tuple-element.289, s32[2048]{0:T(1024)S(1)} %bitcast.126, s32[2048]{0:T(1024)S(1)} %bitcast.127, s32[2048]{0:T(1024)S(1)} %bitcast.128, ...), kind=kOutput, calls=%fused_computation.41.clone.1 | convolution fusion | flops 1105723392 | bytes 2705920 | tf_op jit(solution)/shard_map/while/body/eval_jaxpr/dot_general | solution.py:24
  53.0 0.7 dynamic_slice.22
  54.3 6.6 %fusion.68 = bf16[8,512,512]{2,1,0:T(8,128)(2,1)} fusion(bf16[8,512,512]{2,1,0:T(8,128)(2,1)} %get-tuple-element.280, s32[]{:T(128)} %get-tuple-element.279, bf16[2048,512]{1,0:T(8,128)(2,1)} %get-tuple-element.289, s32[2048]{0:T(1024)S(1)} %bitcast.126, s32[2048]{0:T(1024)S(1)} %bitcast.127, s32[2048]{0:T(1024)S(1)} %bitcast.128, ...), kind=kOutput, calls=%fused_computation.41.clone.1 | convolution fusion | flops 1105723392 | bytes 2705920 | tf_op jit(solution)/shard_map/while/body/eval_jaxpr/dot_general | solution.py:24
  60.9 0.7 dynamic_slice.22
  61.6 0.6 iota_add_fusion.5
  62.2 6.6 %fusion.68 = bf16[8,512,512]{2,1,0:T(8,128)(2,1)} fusion(bf16[8,512,512]{2,1,0:T(8,128)(2,1)} %get-tuple-element.280, s32[]{:T(128)} %get-tuple-element.279, bf16[2048,512]{1,0:T(8,128)(2,1)} %get-tuple-element.289, s32[2048]{0:T(1024)S(1)} %bitcast.126, s32[2048]{0:T(1024)S(1)} %bitcast.127, s32[2048]{0:T(1024)S(1)} %bitcast.128, ...), kind=kOutput, calls=%fused_computation.41.clone.1 | convolution fusion | flops 1105723392 | bytes 2705920 | tf_op jit(solution)/shard_map/while/body/eval_jaxpr/dot_general | solution.py:24
  68.9 0.7 dynamic_slice.22
  70.1 6.6 %fusion.68 = bf16[8,512,512]{2,1,0:T(8,128)(2,1)} fusion(bf16[8,512,512]{2,1,0:T(8,128)(2,1)} %get-tuple-element.280, s32[]{:T(128)} %get-tuple-element.279, bf16[2048,512]{1,0:T(8,128)(2,1)} %get-tuple-element.289, s32[2048]{0:T(1024)S(1)} %bitcast.126, s32[2048]{0:T(1024)S(1)} %bitcast.127, s32[2048]{0:T(1024)S(1)} %bitcast.128, ...), kind=kOutput, calls=%fused_computation.41.clone.1 | convolution fusion | flops 1105723392 | bytes 2705920 | tf_op jit(solution)/shard_map/while/body/eval_jaxpr/dot_general | solution.py:24
  77.1 4.5 fusion.41
  81.6 39.7 %while.22 = (s32[]{:T(128)}, bf16[4,512,512]{2,1,0:T(8,128)(2,1)}, s32[2048,15]{0,1:T(8,128)S(1)}, s32[4]{0:T(128)S(1)}, bf16[2048,512]{1,0:T(8,128)(2,1)}, /*index=5*/s32[]{:T(128)}) while((s32[]{:T(128)}, bf16[4,512,512]{2,1,0:T(8,128)(2,1)}, s32[2048,15]{0,1:T(8,128)S(1)}, s32[4]{0:T(128)S(1)}, bf16[2048,512]{1,0:T(8,128)(2,1)}, ...), condition=%wide.region_1.2_spmd.clone, body=%wide.region_0.1_spmd.clone.sunk | while | flops 1121452544 | bytes 2994773 | solution.py:28
  82.9 8.6 %fusion.65 = bf16[4,512,512]{2,1,0:T(8,128)(2,1)} fusion(bf16[4,512,512]{2,1,0:T(8,128)(2,1)} %get-tuple-element.262, s32[]{:T(128)} %get-tuple-element.261, bf16[2048,512]{1,0:T(8,128)(2,1)} %get-tuple-element.271, s32[2048]{0:T(1024)S(1)} %bitcast.111, s32[2048]{0:T(1024)S(1)} %bitcast.112, s32[2048]{0:T(1024)S(1)} %bitcast.113, ...), kind=kOutput, calls=%fused_computation.23.clone.1 | convolution fusion | flops 1121452032 | bytes 2746880 | tf_op jit(solution)/shard_map/while/body/eval_jaxpr/dot_general | solution.py:24
  92.8 8.6 %fusion.65 = bf16[4,512,512]{2,1,0:T(8,128)(2,1)} fusion(bf16[4,512,512]{2,1,0:T(8,128)(2,1)} %get-tuple-element.262, s32[]{:T(128)} %get-tuple-element.261, bf16[2048,512]{1,0:T(8,128)(2,1)} %get-tuple-element.271, s32[2048]{0:T(1024)S(1)} %bitcast.111, s32[2048]{0:T(1024)S(1)} %bitcast.112, s32[2048]{0:T(1024)S(1)} %bitcast.113, ...), kind=kOutput, calls=%fused_computation.23.clone.1 | convolution fusion | flops 1121452032 | bytes 2746880 | tf_op jit(solution)/shard_map/while/body/eval_jaxpr/dot_general | solution.py:24
  102.8 8.6 %fusion.65 = bf16[4,512,512]{2,1,0:T(8,128)(2,1)} fusion(bf16[4,512,512]{2,1,0:T(8,128)(2,1)} %get-tuple-element.262, s32[]{:T(128)} %get-tuple-element.261, bf16[2048,512]{1,0:T(8,128)(2,1)} %get-tuple-element.271, s32[2048]{0:T(1024)S(1)} %bitcast.111, s32[2048]{0:T(1024)S(1)} %bitcast.112, s32[2048]{0:T(1024)S(1)} %bitcast.113, ...), kind=kOutput, calls=%fused_computation.23.clone.1 | convolution fusion | flops 1121452032 | bytes 2746880 | tf_op jit(solution)/shard_map/while/body/eval_jaxpr/dot_general | solution.py:24
  112.7 8.6 %fusion.65 = bf16[4,512,512]{2,1,0:T(8,128)(2,1)} fusion(bf16[4,512,512]{2,1,0:T(8,128)(2,1)} %get-tuple-element.262, s32[]{:T(128)} %get-tuple-element.261, bf16[2048,512]{1,0:T(8,128)(2,1)} %get-tuple-element.271, s32[2048]{0:T(1024)S(1)} %bitcast.111, s32[2048]{0:T(1024)S(1)} %bitcast.112, s32[2048]{0:T(1024)S(1)} %bitcast.113, ...), kind=kOutput, calls=%fused_computation.23.clone.1 | convolution fusion | flops 1121452032 | bytes 2746880 | tf_op jit(solution)/shard_map/while/body/eval_jaxpr/dot_general | solution.py:24
  121.3 4.6 fusion.50
  125.9 66.6 %all-reduce.6.cloned.1.call-done = bf16[4096,512]{1,0:T(8,128)(2,1)} async-done(((bf16[4096,512]{1,0:T(8,128)(2,1)}), bf16[4096,512]{1,0:T(8,128)(2,1)}) %all-reduce.6.cloned.1.call-update) | async-done | bytes 4194320 | tf_op jit(solution)/shard_map/psum | solution.py:49
  192.6 3.6 add_bitcast_fusion
  196.2 99.7 %all-reduce.10.cloned.1.call-done = (f32[768,512]{0,1:T(8,128)}, f32[512,512]{1,0:T(8,128)}) async-done(((f32[768,512]{0,1:T(8,128)}, f32[512,512]{1,0:T(8,128)}), (f32[768,512]{0,1:T(8,128)}, f32[512,512]{1,0:T(8,128)})) %all-reduce.10.cloned.1.call-update) | async-done | bytes 2621456 | tf_op jit(solution)/shard_map/psum | solution.py:8
  296.0 237.0 %all-reduce.8.cloned.1.call-done = (f32[768,512]{0,1:T(8,128)}, f32[512,512]{1,0:T(8,128)}) async-done(((f32[768,512]{0,1:T(8,128)}, f32[512,512]{1,0:T(8,128)}), (f32[768,512]{0,1:T(8,128)}, f32[512,512]{1,0:T(8,128)})) %all-reduce.8.cloned.1.call-update) | async-done | bytes 2621456 | tf_op jit(solution)/shard_map/psum | solution.py:9
  533.0 3.0 copy.10
  536.0 2.3 copy.32
  (44 shorter events, 10.3 us)
Async XLA Ops:
  7.2 114.2 %copy-start = (bf16[2048,768]{1,0:T(8,128)(2,1)S(1)}, bf16[2048,768]{1,0:T(8,128)(2,1)}, u32[]{:S(2)}) copy-start(bf16[2048,768]{1,0:T(8,128)(2,1)} %param.19) | copy-start | bytes 9437188
  7.2 185.4 %all-reduce.6.cloned.1.call-start = ((), (), s32[]{:S(2)}) async-start(), calls=%async_computation | async-start | bytes 8388608 | tf_op jit(solution)/shard_map/psum | solution.py:49
  8.1 5.2 copy-start.2
  76.8 4.8 copy-start.1
  76.8 219.1 %all-reduce.10.cloned.1.call-start = ((), (), s32[]{:S(2)}) async-start(), calls=%async_computation.2 | async-start | bytes 5242880 | tf_op jit(solution)/shard_map/psum | solution.py:8
  196.2 336.8 %all-reduce.8.cloned.1.call-start = ((), (), s32[]{:S(2)}) async-start(), calls=%async_computation.1 | async-start | bytes 5242880 | tf_op jit(solution)/shard_map/psum | solution.py:9
Sparse Core Ops, SparseCore 0:
  76.9 115.6 all-reduce.5
  196.3 99.6 all-reduce.9
  298.6 234.3 all-reduce.7
